TPU v7x, 32 devices: a whole 2x2x4 slice. The times are simulated.
32 devices in a mesh: sky: 2 (over x), vel: 16 (over z, y, core).
Axes of the slice: x: 2, y: 2, z: 4, core: 2. Of those that a mesh axis runs over, the one named last changes fastest.
Arguments:
- psi: bfloat16 [2, 512, 1024], P(None, 'vel', 'sky'), may hold values from -6 to 6
- phi: bfloat16 [2, 512, 1024], P(None, 'vel', 'sky'), may hold values from 0.25 to 4
- shifts: int32 [512, 2, 2], P('vel'), may hold values from -16 to 16, as said below
- tile_mask: int32 [2, 2], replicated, may hold values 0 or 1
Outputs:
- best: float32 [512, 1024], P('vel', 'sky')
Inputs may be any that keep to these rules, and one draw needn't show every extreme that they name: `shifts`: pixel offsets of an epoch's image; entry 0 is a row offset, entry 1 a column offset.
All inputs are finite; a program needn't handle non-finite values.
Results may differ from a plain program's by a relative error of at most 0.0003.
Values may be sent and summed in bfloat16 or wider, within the bound.
No kernel may reach another device: no remote copies, remote signals or barrier semaphores. Data moves between devices by JAX's collectives and lax.ppermute only.
A program may use at most 64 MiB of HBM per device.

v0:
```python
import jax
import jax.numpy as jnp
from jax import lax
from jax.sharding import PartitionSpec as P

MAXS = 16


def padded_2(block, sides, width):
    for axis, dim in sides:
        count = lax.axis_size(axis)
        forward = [(i, i + 1) for i in range(count - 1)]
        backward = [(target, source) for source, target in forward]
        low = lax.ppermute(
            lax.slice_in_dim(block, block.shape[dim] - width, None, axis=dim), axis, forward
        )
        high = lax.ppermute(lax.slice_in_dim(block, 0, width, axis=dim), axis, backward)
        block = jnp.concatenate([low, block, high], axis=dim)
    return block


def stack_best(padded, offset_table, height, breadth, margin):
    total_vel = offset_table.shape[0]
    epochs = padded.shape[1]
    per_step = 1
    while total_vel // per_step > 16 or total_vel % per_step:
        per_step += 1
    grouped = offset_table.reshape(total_vel // per_step, per_step, epochs, 2)

    def advance(record, offsets):
        for member in range(per_step):
            psi_total = jnp.zeros((height, breadth), jnp.float32)
            phi_total = jnp.zeros((height, breadth), jnp.float32)
            for epoch in range(epochs):
                row_at = margin + offsets[member, epoch, 0]
                col_at = margin + offsets[member, epoch, 1]
                psi_total = psi_total + lax.dynamic_slice(
                    padded[0, epoch], (row_at, col_at), (height, breadth)
                ).astype(jnp.float32)
                phi_total = phi_total + lax.dynamic_slice(
                    padded[1, epoch], (row_at, col_at), (height, breadth)
                ).astype(jnp.float32)
            record = jnp.maximum(record, psi_total / jnp.sqrt(jnp.maximum(phi_total, 1.0)))
        return (record, None)

    start = jnp.full((height, breadth), -1e30, jnp.float32)
    record, unused = lax.scan(advance, start, grouped)
    return record


def body(psi, phi, shifts, tile_mask):
    margin = MAXS
    height = psi.shape[1]
    breadth = psi.shape[2]
    sky_index = lax.axis_index("sky")
    keep = lax.dynamic_slice_in_dim(tile_mask, sky_index, 1, 1).astype(jnp.bfloat16)[:, :, None]
    stacked = jnp.stack([psi * keep, phi * keep])
    whole = lax.all_gather(stacked, "vel", axis=2, tiled=True)
    rimmed = padded_2(whole, (("sky", 3),), margin)
    padded = jnp.pad(rimmed, ((0, 0), (0, 0), (margin, margin), (0, 0)))
    full_height = rimmed.shape[2]
    record = stack_best(padded, shifts, full_height, breadth, margin)
    joined = lax.pmax(record, "vel")
    result = lax.dynamic_slice_in_dim(joined, lax.axis_index("vel") * height, height, 0)
    return result


def solution(mesh):
    placed = (P(None, "vel", "sky"), P(None, "vel", "sky"), P("vel", None, None), P())
    return jax.shard_map(
        body, mesh=mesh, in_specs=placed, out_specs=P("vel", "sky"), check_vma=False
    )
```

profile of v0, /device:TPU:0, one launch (start us, length us, event | category | flops | bytes accessed | tf_op | source)
XLA Modules:
  0.0 437.1 jit_solution(14862448438077397219)
XLA Ops:
  6.5 0.9 fusion.7
  7.4 1.0 multiply_bitcast_fusion.1
  8.4 0.7 pad_maximum_fusion
  9.1 44.6 %all-gather.2.cloned.1.call-done = bf16[2,2,512,512]{3,2,1,0:T(8,128)(2,1)} async-done(((bf16[2,2,32,512]{3,2,1,0:T(8,128)(2,1)}), bf16[2,2,512,512]{3,2,1,0:T(8,128)(2,1)}) %all-gather.2.cloned.1.call-update) | async-done | bytes 2097168 | tf_op jit(solution)/shard_map/all_gather | solution.py:58
  53.7 1.4 fusion.10
  55.1 3.4 collective-permute-start
  58.5 1.3 collective-permute-start.1
  60.0 10.1 %collective-permute-done = bf16[2,2,512,16]{3,2,1,0:T(8,128)(2,1)S(1)} collective-permute-done((bf16[2,2,512,16]{3,2,1,0:T(8,128)(2,1)S(1)}, bf16[2,2,512,16]{3,2,1,0:T(8,128)(2,1)S(1)}, u32[]{:S(2)}, u32[]{:S(2)}) %collective-permute-start) | collective-permute-done | bytes 65568 | tf_op jit(solution)/shard_map/ppermute | solution.py:14
  70.1 4.3 collective-permute-done.1
  74.4 3.1 fusion.6
  77.5 259.4 %while.14 = (s32[]{:T(128)}, f32[512,512]{1,0:T(8,128)}, bf16[2,2,544,544]{3,2,1,0:T(8,128)(2,1)S(1)}, s32[16,2,2,2]{3,2,1,0:T(2,128)S(1)}, s32[]{:T(128)}, /*in...) while((s32[]{:T(128)}, f32[512,512]{1,0:T(8,128)}, bf16[2,2,544,544]{3,2,1,0:T(8,128)(2,1)S(1)}, ...), condition=%wide.region_1.2_spmd.clone, body=%wide.region_0.1_spmd.clone.sunk | while | flops 4980771 | bytes 19415732 | solution.py:47
  77.5 0.7 fusion.16
  88.2 1.0 copy-done
  89.2 3.5 bitcast_maximum_fusion.3
  92.7 1.0 copy-done.1
  104.4 1.0 copy-done
  105.4 3.5 bitcast_maximum_fusion.3
  108.9 1.0 copy-done.1
  109.9 0.7 fusion.16
  120.6 1.0 copy-done
  121.6 3.5 bitcast_maximum_fusion.3
  125.1 1.0 copy-done.1
  136.8 1.0 copy-done
  137.8 3.5 bitcast_maximum_fusion.3
  141.4 1.0 copy-done.1
  153.0 1.0 copy-done
  154.0 3.5 bitcast_maximum_fusion.3
  157.5 1.0 copy-done.1
  158.5 0.7 fusion.16
  169.2 1.0 copy-done
  170.2 3.5 bitcast_maximum_fusion.3
  173.7 1.0 copy-done.1
  185.4 1.0 copy-done
  186.4 3.5 bitcast_maximum_fusion.3
  189.9 1.0 copy-done.1
  201.6 1.0 copy-done
  202.6 3.5 bitcast_maximum_fusion.3
  206.2 1.0 copy-done.1
  217.8 1.0 copy-done
  218.8 3.5 bitcast_maximum_fusion.3
  222.4 1.0 copy-done.1
  234.1 1.0 copy-done
  235.0 3.6 bitcast_maximum_fusion.3
  238.6 1.0 copy-done.1
  250.3 1.0 copy-done
  251.3 3.6 bitcast_maximum_fusion.3
  254.8 1.0 copy-done.1
  266.5 1.0 copy-done
  267.5 3.5 bitcast_maximum_fusion.3
  271.0 1.0 copy-done.1
  282.7 1.0 copy-done
  283.7 3.5 bitcast_maximum_fusion.3
  287.2 1.0 copy-done.1
  298.9 1.0 copy-done
  299.9 3.5 bitcast_maximum_fusion.3
  303.4 1.0 copy-done.1
  315.1 1.0 copy-done
  316.1 3.5 bitcast_maximum_fusion.3
  319.6 1.0 copy-done.1
  331.3 1.0 copy-done
  332.3 3.5 bitcast_maximum_fusion.3
  335.9 1.0 copy-done.1
  336.9 91.9 %all-reduce.3.cloned.1.call-done = f32[512,512]{1,0:T(8,128)} async-done(((f32[512,512]{1,0:T(8,128)}), f32[512,512]{1,0:T(8,128)}) %all-reduce.3.cloned.1.call-update) | async-done | bytes 1048592 | tf_op jit(solution)/shard_map/pmax | solution.py:63
  428.8 1.5 constant_dynamic-slice_fusion.1
  (85 shorter events, 12.6 us)
Async XLA Ops:
  6.5 53.3 %copy-start.2 = (s32[32,2,2]{0,2,1:T(2,128)S(1)}, s32[32,2,2]{0,2,1:T(2,128)}, u32[]{:S(2)}) copy-start(s32[32,2,2]{0,2,1:T(2,128)} %param.8) | copy-start | bytes 1540
  6.5 47.2 %all-gather.2.cloned.1.call-start = ((), (), s32[]{:S(2)}) async-start(), calls=%async_computation | async-start | bytes 2228224 | tf_op jit(solution)/shard_map/all_gather | solution.py:58
  9.1 419.7 %all-reduce.3.cloned.1.call-start = ((), (), s32[]{:S(2)}) async-start(), calls=%async_computation.1 | async-start | bytes 2097152 | tf_op jit(solution)/shard_map/pmax | solution.py:63
  55.1 15.0 %collective-permute-start = (bf16[2,2,512,16]{3,2,1,0:T(8,128)(2,1)S(1)}, bf16[2,2,512,16]{3,2,1,0:T(8,128)(2,1)S(1)}, u32[]{:S(2)}, u32[]{:S(2)}) collective-permute-start(bf16[2,2,512,16]{3,2,1,0:T(8,128)(2,1)S(1)} %get-tuple-element.122), channel_id=1, source_target_pairs={{0,16},{1,17},{2,18},{3,19},{4,20},{5,21},{6,22},{7,23},{8,24},{9,... | collective-permute-start | bytes 196616 | tf_op jit(solution)/shard_map/ppermute | solution.py:14
  58.5 15.8 %collective-permute-start.1 = (bf16[2,2,512,16]{3,2,1,0:T(8,128)(2,1)S(1)}, bf16[2,2,512,16]{3,2,1,0:T(8,128)(2,1)}, u32[]{:S(2)}, u32[]{:S(2)}) collective-permute-start(bf16[2,2,512,16]{3,2,1,0:T(8,128)(2,1)S(1)} %get-tuple-element.123), channel_id=1, source_target_pairs={{16,0},{17,1},{18,2},{19,3},{20,4},{21,5},{22,6},{23,7},{24,8},{25... | collective-permute-start | bytes 196616 | tf_op jit(solution)/shard_map/ppermute | solution.py:17
  88.0 1.2 copy-start
  92.7 1.0 copy-start.1
  104.2 1.2 copy-start
  108.9 1.0 copy-start.1
  120.4 1.2 copy-start
  125.1 1.0 copy-start.1
  136.6 1.2 copy-start
  141.3 1.0 copy-start.1
  152.8 1.2 copy-start
  157.5 1.0 copy-start.1
  169.0 1.2 copy-start
  173.7 1.0 copy-start.1
  185.2 1.2 copy-start
  189.9 1.0 copy-start.1
  201.4 1.2 copy-start
  206.1 1.0 copy-start.1
  217.6 1.2 copy-start
  222.4 1.0 copy-start.1
  233.8 1.2 copy-start
  238.6 1.0 copy-start.1
  250.0 1.2 copy-start
  254.8 1.0 copy-start.1
  266.2 1.2 copy-start
  271.0 1.0 copy-start.1
  282.5 1.2 copy-start
  287.2 1.0 copy-start.1
  298.7 1.2 copy-start
  303.4 1.0 copy-start.1
  314.9 1.2 copy-start
  319.6 1.0 copy-start.1
  331.1 1.2 copy-start
  335.8 1.0 copy-start.1
Sparse Core Ops, SparseCore 0:
  9.5 44.1 all-gather.1
  337.0 91.7 all-reduce.2
where the time goes:
time: 440 us; the launch traced here: 437 us
  loops' own time  157 us (36%)
  waiting for transfers between devices  151 us (34%)
  other arithmetic  62.2 us (14%)
  local copies, waits for them, and re-layouts  48.6 us (11%)
  between operations  13.5 us (3%)
  starting transfers between devices  4.74 us (1%)
    another operation x1, loops' own time, stack_best(): record, unused = lax.scan(advance, start, grouped)  157 us
    pmax x1, waiting for transfers between devices, body(): joined = lax.pmax(record, 'vel')  91.9 us
    max x16, other arithmetic, advance(): jnp.maximum(record, psi_total / jnp.sqrt(jnp.maximum(phi_total, 1.0)))  56.6 us
    all_gather x1, waiting for transfers between devices, body(): whole = lax.all_gather(stacked, 'vel', axis=2, tiled=True)  44.6 us
    while x64, local copies, waits for them, and re-layouts  31.2 us
    slice x16, local copies, waits for them, and re-layouts, advance(): col_at = margin + offsets[member, epoch, 1]  10.5 us
    ppermute x1, waiting for transfers between devices, padded_2(): lax.ppermute(lax.slice_in_dim(block, block.shape[dim] - width, None, axis...  10.1 us
  transfers between devices with their start and end apart: 4, of which 4 were waited for; matrix products, arithmetic and copies ran while one was open for 0% of the time, Pallas kernels for 0%

commit v1 on v0

--- a/solution.py
+++ b/solution.py
@@ -55,7 +55,12 @@
     sky_index = lax.axis_index("sky")
     keep = lax.dynamic_slice_in_dim(tile_mask, sky_index, 1, 1).astype(jnp.bfloat16)[:, :, None]
     stacked = jnp.stack([psi * keep, phi * keep])
-    whole = lax.all_gather(stacked, "vel", axis=2, tiled=True)
+    ring = [stacked]
+    for hop in range(15):
+        ring.append(lax.ppermute(ring[-1], "vel", [(dev, (dev + 1) % 16) for dev in range(16)]))
+    whole = jnp.roll(
+        jnp.concatenate(ring[::-1], axis=2), (lax.axis_index("vel") + 1) * ring[0].shape[2], axis=2
+    )
     rimmed = padded_2(whole, (("sky", 3),), margin)
     padded = jnp.pad(rimmed, ((0, 0), (0, 0), (margin, margin), (0, 0)))
     full_height = rimmed.shape[2]

time: 440 us -> 528 us (1.20)
  waiting for transfers between devices: 151 us -> 206 us
  other arithmetic: 62.2 us -> 95.6 us
    ppermute x0 -> x15, waiting for transfers between devices: none -> 106 us  [body(): lax.ppermute(ring[-1], 'vel', [(dev, (dev + 1) % 16) for dev in range(16)])]
    all_gather x1 -> x0, waiting for transfers between devices: 44.6 us -> none  [body(): whole = lax.all_gather(stacked, 'vel', axis=2, tiled=True)]
    max x16, other arithmetic: 56.6 us -> 90.8 us  [advance(): jnp.maximum(record, psi_total / jnp.sqrt(jnp.maximum(phi_total, 1.0)))]
    while x64 -> x0, local copies, waits for them, and re-layouts: 31.2 us -> none
    slice x16, local copies, waits for them, and re-layouts: 3.87 us -> 31.6 us  [advance(): padded[0, epoch]]
  transfers between devices with their start and end apart: 4 -> 18, of which waited for: 4 -> 18; matrix products, arithmetic and copies ran while one was open for 0% -> 0% of each run, Pallas kernels for 0% -> 0%
where the time goes in v1:
time: 528 us; the launch traced here: 524 us
  waiting for transfers between devices  206 us (39%)
  loops' own time  158 us (30%)
  other arithmetic  95.6 us (18%)
  local copies, waits for them, and re-layouts  45.5 us (9%)
  between operations  13.7 us (3%)
  starting transfers between devices  5.7 us (1%)
    another operation x1, loops' own time, stack_best(): record, unused = lax.scan(advance, start, grouped)  158 us
    ppermute x15, waiting for transfers between devices, body(): lax.ppermute(ring[-1], 'vel', [(dev, (dev + 1) % 16) for dev in range(16)])  106 us
    max x16, other arithmetic, advance(): jnp.maximum(record, psi_total / jnp.sqrt(jnp.maximum(phi_total, 1.0)))  90.8 us
    pmax x1, waiting for transfers between devices, body(): joined = lax.pmax(record, 'vel')  90.1 us
    slice x16, local copies, waits for them, and re-layouts, advance(): padded[0, epoch]  31.6 us
    slice x16, local copies, waits for them, and re-layouts, advance(): col_at = margin + offsets[member, epoch, 1]  10.9 us
  transfers between devices with their start and end apart: 18, of which 18 were waited for; matrix products, arithmetic and copies ran while one was open for 0% of the time, Pallas kernels for 0%

profile of v1, /device:TPU:0, one launch (start us, length us, event | category | flops | bytes accessed | tf_op | source)
XLA Modules:
  0.0 524.2 jit_solution(6732705180513405737)
XLA Ops:
  6.5 0.9 fusion.8
  7.4 1.0 multiply_bitcast_fusion.1
  8.9 7.6 %collective-permute-done = bf16[2,2,32,512]{3,2,1,0:T(8,128)(2,1)S(1)} collective-permute-done((bf16[2,2,32,512]{3,2,1,0:T(8,128)(2,1)S(1)}, bf16[2,2,32,512]{3,2,1,0:T(8,128)(2,1)S(1)}, u32[]{:S(2)}, u32[]{:S(2)}) %collective-permute-start) | collective-permute-done | bytes 131104 | tf_op jit(solution)/shard_map/ppermute | solution.py:60
  16.5 7.1 %collective-permute-done.1 = bf16[2,2,32,512]{3,2,1,0:T(8,128)(2,1)S(1)} collective-permute-done((bf16[2,2,32,512]{3,2,1,0:T(8,128)(2,1)S(1)}, bf16[2,2,32,512]{3,2,1,0:T(8,128)(2,1)S(1)}, u32[]{:S(2)}, u32[]{:S(2)}) %collective-permute-start.1) | collective-permute-done | bytes 131104 | tf_op jit(solution)/shard_map/ppermute | solution.py:60
  23.6 7.1 %collective-permute-done.2 = bf16[2,2,32,512]{3,2,1,0:T(8,128)(2,1)S(1)} collective-permute-done((bf16[2,2,32,512]{3,2,1,0:T(8,128)(2,1)S(1)}, bf16[2,2,32,512]{3,2,1,0:T(8,128)(2,1)S(1)}, u32[]{:S(2)}, u32[]{:S(2)}) %collective-permute-start.2) | collective-permute-done | bytes 131104 | tf_op jit(solution)/shard_map/ppermute | solution.py:60
  30.7 7.1 %collective-permute-done.3 = bf16[2,2,32,512]{3,2,1,0:T(8,128)(2,1)S(1)} collective-permute-done((bf16[2,2,32,512]{3,2,1,0:T(8,128)(2,1)S(1)}, bf16[2,2,32,512]{3,2,1,0:T(8,128)(2,1)S(1)}, u32[]{:S(2)}, u32[]{:S(2)}) %collective-permute-start.3) | collective-permute-done | bytes 131104 | tf_op jit(solution)/shard_map/ppermute | solution.py:60
  37.8 7.1 %collective-permute-done.4 = bf16[2,2,32,512]{3,2,1,0:T(8,128)(2,1)S(1)} collective-permute-done((bf16[2,2,32,512]{3,2,1,0:T(8,128)(2,1)S(1)}, bf16[2,2,32,512]{3,2,1,0:T(8,128)(2,1)S(1)}, u32[]{:S(2)}, u32[]{:S(2)}) %collective-permute-start.4) | collective-permute-done | bytes 131104 | tf_op jit(solution)/shard_map/ppermute | solution.py:60
  44.9 7.1 %collective-permute-done.5 = bf16[2,2,32,512]{3,2,1,0:T(8,128)(2,1)S(1)} collective-permute-done((bf16[2,2,32,512]{3,2,1,0:T(8,128)(2,1)S(1)}, bf16[2,2,32,512]{3,2,1,0:T(8,128)(2,1)S(1)}, u32[]{:S(2)}, u32[]{:S(2)}) %collective-permute-start.5) | collective-permute-done | bytes 131104 | tf_op jit(solution)/shard_map/ppermute | solution.py:60
  52.0 7.1 %collective-permute-done.6 = bf16[2,2,32,512]{3,2,1,0:T(8,128)(2,1)S(1)} collective-permute-done((bf16[2,2,32,512]{3,2,1,0:T(8,128)(2,1)S(1)}, bf16[2,2,32,512]{3,2,1,0:T(8,128)(2,1)S(1)}, u32[]{:S(2)}, u32[]{:S(2)}) %collective-permute-start.6) | collective-permute-done | bytes 131104 | tf_op jit(solution)/shard_map/ppermute | solution.py:60
  59.1 7.1 %collective-permute-done.7 = bf16[2,2,32,512]{3,2,1,0:T(8,128)(2,1)S(1)} collective-permute-done((bf16[2,2,32,512]{3,2,1,0:T(8,128)(2,1)S(1)}, bf16[2,2,32,512]{3,2,1,0:T(8,128)(2,1)S(1)}, u32[]{:S(2)}, u32[]{:S(2)}) %collective-permute-start.7) | collective-permute-done | bytes 131104 | tf_op jit(solution)/shard_map/ppermute | solution.py:60
  66.2 7.1 %collective-permute-done.8 = bf16[2,2,32,512]{3,2,1,0:T(8,128)(2,1)S(1)} collective-permute-done((bf16[2,2,32,512]{3,2,1,0:T(8,128)(2,1)S(1)}, bf16[2,2,32,512]{3,2,1,0:T(8,128)(2,1)S(1)}, u32[]{:S(2)}, u32[]{:S(2)}) %collective-permute-start.8) | collective-permute-done | bytes 131104 | tf_op jit(solution)/shard_map/ppermute | solution.py:60
  73.3 7.1 %collective-permute-done.9 = bf16[2,2,32,512]{3,2,1,0:T(8,128)(2,1)S(1)} collective-permute-done((bf16[2,2,32,512]{3,2,1,0:T(8,128)(2,1)S(1)}, bf16[2,2,32,512]{3,2,1,0:T(8,128)(2,1)S(1)}, u32[]{:S(2)}, u32[]{:S(2)}) %collective-permute-start.9) | collective-permute-done | bytes 131104 | tf_op jit(solution)/shard_map/ppermute | solution.py:60
  80.3 7.1 %collective-permute-done.10 = bf16[2,2,32,512]{3,2,1,0:T(8,128)(2,1)S(1)} collective-permute-done((bf16[2,2,32,512]{3,2,1,0:T(8,128)(2,1)S(1)}, bf16[2,2,32,512]{3,2,1,0:T(8,128)(2,1)S(1)}, u32[]{:S(2)}, u32[]{:S(2)}) %collective-permute-start.10) | collective-permute-done | bytes 131104 | tf_op jit(solution)/shard_map/ppermute | solution.py:60
  87.4 7.1 %collective-permute-done.11 = bf16[2,2,32,512]{3,2,1,0:T(8,128)(2,1)S(1)} collective-permute-done((bf16[2,2,32,512]{3,2,1,0:T(8,128)(2,1)S(1)}, bf16[2,2,32,512]{3,2,1,0:T(8,128)(2,1)S(1)}, u32[]{:S(2)}, u32[]{:S(2)}) %collective-permute-start.11) | collective-permute-done | bytes 131104 | tf_op jit(solution)/shard_map/ppermute | solution.py:60
  94.5 7.1 %collective-permute-done.12 = bf16[2,2,32,512]{3,2,1,0:T(8,128)(2,1)S(1)} collective-permute-done((bf16[2,2,32,512]{3,2,1,0:T(8,128)(2,1)S(1)}, bf16[2,2,32,512]{3,2,1,0:T(8,128)(2,1)S(1)}, u32[]{:S(2)}, u32[]{:S(2)}) %collective-permute-start.12) | collective-permute-done | bytes 131104 | tf_op jit(solution)/shard_map/ppermute | solution.py:60
  101.6 7.1 %collective-permute-done.13 = bf16[2,2,32,512]{3,2,1,0:T(8,128)(2,1)S(1)} collective-permute-done((bf16[2,2,32,512]{3,2,1,0:T(8,128)(2,1)S(1)}, bf16[2,2,32,512]{3,2,1,0:T(8,128)(2,1)S(1)}, u32[]{:S(2)}, u32[]{:S(2)}) %collective-permute-start.13) | collective-permute-done | bytes 131104 | tf_op jit(solution)/shard_map/ppermute | solution.py:60
  108.7 0.8 copy.7
  109.5 6.3 %collective-permute-done.14 = bf16[2,2,32,512]{3,2,1,0:T(8,128)(2,1)S(1)} collective-permute-done((bf16[2,2,32,512]{3,2,1,0:T(8,128)(2,1)S(1)}, bf16[2,2,32,512]{3,2,1,0:T(8,128)(2,1)S(1)}, u32[]{:S(2)}, u32[]{:S(2)}) %collective-permute-start.14) | collective-permute-done | bytes 131104 | tf_op jit(solution)/shard_map/ppermute | solution.py:60
  116.7 3.9 collective-permute-start.15
  120.6 1.3 collective-permute-start.16
  122.0 5.2 collective-permute-done.15
  127.2 4.4 collective-permute-done.16
  131.7 2.9 fusion.6
  134.6 291.2 %while.14 = (s32[]{:T(128)}, f32[512,512]{1,0:T(8,128)}, bf16[2,2,544,544]{3,2,1,0:T(8,128)(2,1)}, s32[16,2,2,2]{3,2,1,0:T(2,128)S(1)}, s32[]{:T(128)}, /*index=...) while((s32[]{:T(128)}, f32[512,512]{1,0:T(8,128)}, bf16[2,2,544,544]{3,2,1,0:T(8,128)(2,1)}, ...), condition=%wide.region_1.2_spmd.clone, body=%wide.region_0.1_spmd.clone.sunk | while | flops 4980771 | bytes 11027059 | solution.py:47
  134.6 0.7 fusion.16
  145.1 2.0 fusion.14
  147.1 4.5 bitcast_maximum_fusion.3
  151.6 0.7 fusion.16
  162.2 2.0 fusion.14
  164.1 5.8 %bitcast_maximum_fusion.3 = f32[512,512]{1,0:T(8,128)} fusion(f32[512,512]{1,0:T(8,128)} %get-tuple-element.184, bf16[1,1,544,544]{3,2,1,0:T(8,128)(2,1)S(1)} %get-tuple-element.163, s32[]{:T(128)S(6)} %select_n.103, s32[]{:T(128)S(6)} %select_n.104, bf16[1,1,544,544]{3,2,1,0:T(8,128)(2,1)S(1)} %get-tuple-element.166, s32[]{:T(128)S(6)} %select_n.105, ...), kind=kLoop, calls=%fused_computation.clone.1 | loop fusion | flops 4980736 | bytes 6291489 | tf_op jit(solution)/shard_map/while/body/eval_jaxpr/max | solution.py:43
  169.9 0.7 fusion.16
  180.4 2.0 fusion.14
  182.4 5.7 %bitcast_maximum_fusion.3 = f32[512,512]{1,0:T(8,128)} fusion(f32[512,512]{1,0:T(8,128)} %get-tuple-element.184, bf16[1,1,544,544]{3,2,1,0:T(8,128)(2,1)S(1)} %get-tuple-element.163, s32[]{:T(128)S(6)} %select_n.103, s32[]{:T(128)S(6)} %select_n.104, bf16[1,1,544,544]{3,2,1,0:T(8,128)(2,1)S(1)} %get-tuple-element.166, s32[]{:T(128)S(6)} %select_n.105, ...), kind=kLoop, calls=%fused_computation.clone.1 | loop fusion | flops 4980736 | bytes 6291489 | tf_op jit(solution)/shard_map/while/body/eval_jaxpr/max | solution.py:43
  188.2 0.7 fusion.16
  198.7 2.0 fusion.14
  200.7 5.8 %bitcast_maximum_fusion.3 = f32[512,512]{1,0:T(8,128)} fusion(f32[512,512]{1,0:T(8,128)} %get-tuple-element.184, bf16[1,1,544,544]{3,2,1,0:T(8,128)(2,1)S(1)} %get-tuple-element.163, s32[]{:T(128)S(6)} %select_n.103, s32[]{:T(128)S(6)} %select_n.104, bf16[1,1,544,544]{3,2,1,0:T(8,128)(2,1)S(1)} %get-tuple-element.166, s32[]{:T(128)S(6)} %select_n.105, ...), kind=kLoop, calls=%fused_computation.clone.1 | loop fusion | flops 4980736 | bytes 6291489 | tf_op jit(solution)/shard_map/while/body/eval_jaxpr/max | solution.py:43
  217.0 2.0 fusion.14
  219.0 5.8 %bitcast_maximum_fusion.3 = f32[512,512]{1,0:T(8,128)} fusion(f32[512,512]{1,0:T(8,128)} %get-tuple-element.184, bf16[1,1,544,544]{3,2,1,0:T(8,128)(2,1)S(1)} %get-tuple-element.163, s32[]{:T(128)S(6)} %select_n.103, s32[]{:T(128)S(6)} %select_n.104, bf16[1,1,544,544]{3,2,1,0:T(8,128)(2,1)S(1)} %get-tuple-element.166, s32[]{:T(128)S(6)} %select_n.105, ...), kind=kLoop, calls=%fused_computation.clone.1 | loop fusion | flops 4980736 | bytes 6291489 | tf_op jit(solution)/shard_map/while/body/eval_jaxpr/max | solution.py:43
  235.3 2.0 fusion.14
  237.3 5.8 %bitcast_maximum_fusion.3 = f32[512,512]{1,0:T(8,128)} fusion(f32[512,512]{1,0:T(8,128)} %get-tuple-element.184, bf16[1,1,544,544]{3,2,1,0:T(8,128)(2,1)S(1)} %get-tuple-element.163, s32[]{:T(128)S(6)} %select_n.103, s32[]{:T(128)S(6)} %select_n.104, bf16[1,1,544,544]{3,2,1,0:T(8,128)(2,1)S(1)} %get-tuple-element.166, s32[]{:T(128)S(6)} %select_n.105, ...), kind=kLoop, calls=%fused_computation.clone.1 | loop fusion | flops 4980736 | bytes 6291489 | tf_op jit(solution)/shard_map/while/body/eval_jaxpr/max | solution.py:43
  253.6 2.0 fusion.14
  255.5 5.8 %bitcast_maximum_fusion.3 = f32[512,512]{1,0:T(8,128)} fusion(f32[512,512]{1,0:T(8,128)} %get-tuple-element.184, bf16[1,1,544,544]{3,2,1,0:T(8,128)(2,1)S(1)} %get-tuple-element.163, s32[]{:T(128)S(6)} %select_n.103, s32[]{:T(128)S(6)} %select_n.104, bf16[1,1,544,544]{3,2,1,0:T(8,128)(2,1)S(1)} %get-tuple-element.166, s32[]{:T(128)S(6)} %select_n.105, ...), kind=kLoop, calls=%fused_computation.clone.1 | loop fusion | flops 4980736 | bytes 6291489 | tf_op jit(solution)/shard_map/while/body/eval_jaxpr/max | solution.py:43
  271.9 2.0 fusion.14
  273.8 5.7 %bitcast_maximum_fusion.3 = f32[512,512]{1,0:T(8,128)} fusion(f32[512,512]{1,0:T(8,128)} %get-tuple-element.184, bf16[1,1,544,544]{3,2,1,0:T(8,128)(2,1)S(1)} %get-tuple-element.163, s32[]{:T(128)S(6)} %select_n.103, s32[]{:T(128)S(6)} %select_n.104, bf16[1,1,544,544]{3,2,1,0:T(8,128)(2,1)S(1)} %get-tuple-element.166, s32[]{:T(128)S(6)} %select_n.105, ...), kind=kLoop, calls=%fused_computation.clone.1 | loop fusion | flops 4980736 | bytes 6291489 | tf_op jit(solution)/shard_map/while/body/eval_jaxpr/max | solution.py:43
  279.6 0.7 fusion.16
  290.1 2.0 fusion.14
  292.1 5.8 %bitcast_maximum_fusion.3 = f32[512,512]{1,0:T(8,128)} fusion(f32[512,512]{1,0:T(8,128)} %get-tuple-element.184, bf16[1,1,544,544]{3,2,1,0:T(8,128)(2,1)S(1)} %get-tuple-element.163, s32[]{:T(128)S(6)} %select_n.103, s32[]{:T(128)S(6)} %select_n.104, bf16[1,1,544,544]{3,2,1,0:T(8,128)(2,1)S(1)} %get-tuple-element.166, s32[]{:T(128)S(6)} %select_n.105, ...), kind=kLoop, calls=%fused_computation.clone.1 | loop fusion | flops 4980736 | bytes 6291489 | tf_op jit(solution)/shard_map/while/body/eval_jaxpr/max | solution.py:43
  297.9 0.7 fusion.16
  308.4 2.0 fusion.14
  310.4 5.8 %bitcast_maximum_fusion.3 = f32[512,512]{1,0:T(8,128)} fusion(f32[512,512]{1,0:T(8,128)} %get-tuple-element.184, bf16[1,1,544,544]{3,2,1,0:T(8,128)(2,1)S(1)} %get-tuple-element.163, s32[]{:T(128)S(6)} %select_n.103, s32[]{:T(128)S(6)} %select_n.104, bf16[1,1,544,544]{3,2,1,0:T(8,128)(2,1)S(1)} %get-tuple-element.166, s32[]{:T(128)S(6)} %select_n.105, ...), kind=kLoop, calls=%fused_computation.clone.1 | loop fusion | flops 4980736 | bytes 6291489 | tf_op jit(solution)/shard_map/while/body/eval_jaxpr/max | solution.py:43
  326.7 2.0 fusion.14
  328.6 5.8 %bitcast_maximum_fusion.3 = f32[512,512]{1,0:T(8,128)} fusion(f32[512,512]{1,0:T(8,128)} %get-tuple-element.184, bf16[1,1,544,544]{3,2,1,0:T(8,128)(2,1)S(1)} %get-tuple-element.163, s32[]{:T(128)S(6)} %select_n.103, s32[]{:T(128)S(6)} %select_n.104, bf16[1,1,544,544]{3,2,1,0:T(8,128)(2,1)S(1)} %get-tuple-element.166, s32[]{:T(128)S(6)} %select_n.105, ...), kind=kLoop, calls=%fused_computation.clone.1 | loop fusion | flops 4980736 | bytes 6291489 | tf_op jit(solution)/shard_map/while/body/eval_jaxpr/max | solution.py:43
  344.9 2.0 fusion.14
  346.9 5.8 %bitcast_maximum_fusion.3 = f32[512,512]{1,0:T(8,128)} fusion(f32[512,512]{1,0:T(8,128)} %get-tuple-element.184, bf16[1,1,544,544]{3,2,1,0:T(8,128)(2,1)S(1)} %get-tuple-element.163, s32[]{:T(128)S(6)} %select_n.103, s32[]{:T(128)S(6)} %select_n.104, bf16[1,1,544,544]{3,2,1,0:T(8,128)(2,1)S(1)} %get-tuple-element.166, s32[]{:T(128)S(6)} %select_n.105, ...), kind=kLoop, calls=%fused_computation.clone.1 | loop fusion | flops 4980736 | bytes 6291489 | tf_op jit(solution)/shard_map/while/body/eval_jaxpr/max | solution.py:43
  363.2 2.0 fusion.14
  365.2 5.7 %bitcast_maximum_fusion.3 = f32[512,512]{1,0:T(8,128)} fusion(f32[512,512]{1,0:T(8,128)} %get-tuple-element.184, bf16[1,1,544,544]{3,2,1,0:T(8,128)(2,1)S(1)} %get-tuple-element.163, s32[]{:T(128)S(6)} %select_n.103, s32[]{:T(128)S(6)} %select_n.104, bf16[1,1,544,544]{3,2,1,0:T(8,128)(2,1)S(1)} %get-tuple-element.166, s32[]{:T(128)S(6)} %select_n.105, ...), kind=kLoop, calls=%fused_computation.clone.1 | loop fusion | flops 4980736 | bytes 6291489 | tf_op jit(solution)/shard_map/while/body/eval_jaxpr/max | solution.py:43
  381.5 2.0 fusion.14
  383.4 5.8 %bitcast_maximum_fusion.3 = f32[512,512]{1,0:T(8,128)} fusion(f32[512,512]{1,0:T(8,128)} %get-tuple-element.184, bf16[1,1,544,544]{3,2,1,0:T(8,128)(2,1)S(1)} %get-tuple-element.163, s32[]{:T(128)S(6)} %select_n.103, s32[]{:T(128)S(6)} %select_n.104, bf16[1,1,544,544]{3,2,1,0:T(8,128)(2,1)S(1)} %get-tuple-element.166, s32[]{:T(128)S(6)} %select_n.105, ...), kind=kLoop, calls=%fused_computation.clone.1 | loop fusion | flops 4980736 | bytes 6291489 | tf_op jit(solution)/shard_map/while/body/eval_jaxpr/max | solution.py:43
  399.7 2.0 fusion.14
  401.7 5.7 %bitcast_maximum_fusion.3 = f32[512,512]{1,0:T(8,128)} fusion(f32[512,512]{1,0:T(8,128)} %get-tuple-element.184, bf16[1,1,544,544]{3,2,1,0:T(8,128)(2,1)S(1)} %get-tuple-element.163, s32[]{:T(128)S(6)} %select_n.103, s32[]{:T(128)S(6)} %select_n.104, bf16[1,1,544,544]{3,2,1,0:T(8,128)(2,1)S(1)} %get-tuple-element.166, s32[]{:T(128)S(6)} %select_n.105, ...), kind=kLoop, calls=%fused_computation.clone.1 | loop fusion | flops 4980736 | bytes 6291489 | tf_op jit(solution)/shard_map/while/body/eval_jaxpr/max | solution.py:43
  418.0 2.0 fusion.14
  420.0 5.8 %bitcast_maximum_fusion.3 = f32[512,512]{1,0:T(8,128)} fusion(f32[512,512]{1,0:T(8,128)} %get-tuple-element.184, bf16[1,1,544,544]{3,2,1,0:T(8,128)(2,1)S(1)} %get-tuple-element.163, s32[]{:T(128)S(6)} %select_n.103, s32[]{:T(128)S(6)} %select_n.104, bf16[1,1,544,544]{3,2,1,0:T(8,128)(2,1)S(1)} %get-tuple-element.166, s32[]{:T(128)S(6)} %select_n.105, ...), kind=kLoop, calls=%fused_computation.clone.1 | loop fusion | flops 4980736 | bytes 6291489 | tf_op jit(solution)/shard_map/while/body/eval_jaxpr/max | solution.py:43
  425.8 90.1 %all-reduce.3.cloned.1.call-done = f32[512,512]{1,0:T(8,128)} async-done(((f32[512,512]{1,0:T(8,128)}), f32[512,512]{1,0:T(8,128)}) %all-reduce.3.cloned.1.call-update) | async-done | bytes 1048592 | tf_op jit(solution)/shard_map/pmax | solution.py:68
  515.9 1.5 constant_dynamic-slice_fusion.3
  (79 shorter events, 8.2 us)
Async XLA Ops:
  6.5 509.3 %all-reduce.3.cloned.1.call-start = ((), (), s32[]{:S(2)}) async-start(), calls=%async_computation | async-start | bytes 2097152 | tf_op jit(solution)/shard_map/pmax | solution.py:68
  8.4 8.2 %collective-permute-start = (bf16[2,2,32,512]{3,2,1,0:T(8,128)(2,1)S(1)}, bf16[2,2,32,512]{3,2,1,0:T(8,128)(2,1)S(1)}, u32[]{:S(2)}, u32[]{:S(2)}) collective-permute-start(bf16[2,2,32,512]{3,2,1,0:T(8,128)(2,1)S(1)} %pad_maximum_fusion), channel_id=1, source_target_pairs={{0,1},{1,2},{2,3},{3,4},{4,5},{5,6},{6,7},{7,8},{8,9},{9,10},{10,1... | collective-permute-start | bytes 393224 | tf_op jit(solution)/shard_map/ppermute | solution.py:60
  16.5 7.1 %collective-permute-start.1 = (bf16[2,2,32,512]{3,2,1,0:T(8,128)(2,1)S(1)}, bf16[2,2,32,512]{3,2,1,0:T(8,128)(2,1)S(1)}, u32[]{:S(2)}, u32[]{:S(2)}) collective-permute-start(bf16[2,2,32,512]{3,2,1,0:T(8,128)(2,1)S(1)} %collective-permute-done), channel_id=1, source_target_pairs={{0,1},{1,2},{2,3},{3,4},{4,5},{5,6},{6,7},{7,8},{8,9},{9,10},{10,1... | collective-permute-start | bytes 393224 | tf_op jit(solution)/shard_map/ppermute | solution.py:60
  23.6 7.1 %collective-permute-start.2 = (bf16[2,2,32,512]{3,2,1,0:T(8,128)(2,1)S(1)}, bf16[2,2,32,512]{3,2,1,0:T(8,128)(2,1)S(1)}, u32[]{:S(2)}, u32[]{:S(2)}) collective-permute-start(bf16[2,2,32,512]{3,2,1,0:T(8,128)(2,1)S(1)} %collective-permute-done.1), channel_id=1, source_target_pairs={{0,1},{1,2},{2,3},{3,4},{4,5},{5,6},{6,7},{7,8},{8,9},{9,10},{10,1... | collective-permute-start | bytes 393224 | tf_op jit(solution)/shard_map/ppermute | solution.py:60
  30.7 7.1 %collective-permute-start.3 = (bf16[2,2,32,512]{3,2,1,0:T(8,128)(2,1)S(1)}, bf16[2,2,32,512]{3,2,1,0:T(8,128)(2,1)S(1)}, u32[]{:S(2)}, u32[]{:S(2)}) collective-permute-start(bf16[2,2,32,512]{3,2,1,0:T(8,128)(2,1)S(1)} %collective-permute-done.2), channel_id=1, source_target_pairs={{0,1},{1,2},{2,3},{3,4},{4,5},{5,6},{6,7},{7,8},{8,9},{9,10},{10,1... | collective-permute-start | bytes 393224 | tf_op jit(solution)/shard_map/ppermute | solution.py:60
  37.8 7.1 %collective-permute-start.4 = (bf16[2,2,32,512]{3,2,1,0:T(8,128)(2,1)S(1)}, bf16[2,2,32,512]{3,2,1,0:T(8,128)(2,1)S(1)}, u32[]{:S(2)}, u32[]{:S(2)}) collective-permute-start(bf16[2,2,32,512]{3,2,1,0:T(8,128)(2,1)S(1)} %collective-permute-done.3), channel_id=1, source_target_pairs={{0,1},{1,2},{2,3},{3,4},{4,5},{5,6},{6,7},{7,8},{8,9},{9,10},{10,1... | collective-permute-start | bytes 393224 | tf_op jit(solution)/shard_map/ppermute | solution.py:60
  44.9 7.1 %collective-permute-start.5 = (bf16[2,2,32,512]{3,2,1,0:T(8,128)(2,1)S(1)}, bf16[2,2,32,512]{3,2,1,0:T(8,128)(2,1)S(1)}, u32[]{:S(2)}, u32[]{:S(2)}) collective-permute-start(bf16[2,2,32,512]{3,2,1,0:T(8,128)(2,1)S(1)} %collective-permute-done.4), channel_id=1, source_target_pairs={{0,1},{1,2},{2,3},{3,4},{4,5},{5,6},{6,7},{7,8},{8,9},{9,10},{10,1... | collective-permute-start | bytes 393224 | tf_op jit(solution)/shard_map/ppermute | solution.py:60
  52.0 7.1 %collective-permute-start.6 = (bf16[2,2,32,512]{3,2,1,0:T(8,128)(2,1)S(1)}, bf16[2,2,32,512]{3,2,1,0:T(8,128)(2,1)S(1)}, u32[]{:S(2)}, u32[]{:S(2)}) collective-permute-start(bf16[2,2,32,512]{3,2,1,0:T(8,128)(2,1)S(1)} %collective-permute-done.5), channel_id=1, source_target_pairs={{0,1},{1,2},{2,3},{3,4},{4,5},{5,6},{6,7},{7,8},{8,9},{9,10},{10,1... | collective-permute-start | bytes 393224 | tf_op jit(solution)/shard_map/ppermute | solution.py:60
  59.1 7.1 %collective-permute-start.7 = (bf16[2,2,32,512]{3,2,1,0:T(8,128)(2,1)S(1)}, bf16[2,2,32,512]{3,2,1,0:T(8,128)(2,1)S(1)}, u32[]{:S(2)}, u32[]{:S(2)}) collective-permute-start(bf16[2,2,32,512]{3,2,1,0:T(8,128)(2,1)S(1)} %collective-permute-done.6), channel_id=1, source_target_pairs={{0,1},{1,2},{2,3},{3,4},{4,5},{5,6},{6,7},{7,8},{8,9},{9,10},{10,1... | collective-permute-start | bytes 393224 | tf_op jit(solution)/shard_map/ppermute | solution.py:60
  66.2 7.1 %collective-permute-start.8 = (bf16[2,2,32,512]{3,2,1,0:T(8,128)(2,1)S(1)}, bf16[2,2,32,512]{3,2,1,0:T(8,128)(2,1)S(1)}, u32[]{:S(2)}, u32[]{:S(2)}) collective-permute-start(bf16[2,2,32,512]{3,2,1,0:T(8,128)(2,1)S(1)} %collective-permute-done.7), channel_id=1, source_target_pairs={{0,1},{1,2},{2,3},{3,4},{4,5},{5,6},{6,7},{7,8},{8,9},{9,10},{10,1... | collective-permute-start | bytes 393224 | tf_op jit(solution)/shard_map/ppermute | solution.py:60
  73.3 7.1 %collective-permute-start.9 = (bf16[2,2,32,512]{3,2,1,0:T(8,128)(2,1)S(1)}, bf16[2,2,32,512]{3,2,1,0:T(8,128)(2,1)S(1)}, u32[]{:S(2)}, u32[]{:S(2)}) collective-permute-start(bf16[2,2,32,512]{3,2,1,0:T(8,128)(2,1)S(1)} %collective-permute-done.8), channel_id=1, source_target_pairs={{0,1},{1,2},{2,3},{3,4},{4,5},{5,6},{6,7},{7,8},{8,9},{9,10},{10,1... | collective-permute-start | bytes 393224 | tf_op jit(solution)/shard_map/ppermute | solution.py:60
  80.3 7.1 %collective-permute-start.10 = (bf16[2,2,32,512]{3,2,1,0:T(8,128)(2,1)S(1)}, bf16[2,2,32,512]{3,2,1,0:T(8,128)(2,1)S(1)}, u32[]{:S(2)}, u32[]{:S(2)}) collective-permute-start(bf16[2,2,32,512]{3,2,1,0:T(8,128)(2,1)S(1)} %collective-permute-done.9), channel_id=1, source_target_pairs={{0,1},{1,2},{2,3},{3,4},{4,5},{5,6},{6,7},{7,8},{8,9},{9,10},{10,1... | collective-permute-start | bytes 393224 | tf_op jit(solution)/shard_map/ppermute | solution.py:60
  87.4 7.1 %collective-permute-start.11 = (bf16[2,2,32,512]{3,2,1,0:T(8,128)(2,1)S(1)}, bf16[2,2,32,512]{3,2,1,0:T(8,128)(2,1)S(1)}, u32[]{:S(2)}, u32[]{:S(2)}) collective-permute-start(bf16[2,2,32,512]{3,2,1,0:T(8,128)(2,1)S(1)} %collective-permute-done.10), channel_id=1, source_target_pairs={{0,1},{1,2},{2,3},{3,4},{4,5},{5,6},{6,7},{7,8},{8,9},{9,10},{10,1... | collective-permute-start | bytes 393224 | tf_op jit(solution)/shard_map/ppermute | solution.py:60
  94.5 7.1 %collective-permute-start.12 = (bf16[2,2,32,512]{3,2,1,0:T(8,128)(2,1)S(1)}, bf16[2,2,32,512]{3,2,1,0:T(8,128)(2,1)S(1)}, u32[]{:S(2)}, u32[]{:S(2)}) collective-permute-start(bf16[2,2,32,512]{3,2,1,0:T(8,128)(2,1)S(1)} %collective-permute-done.11), channel_id=1, source_target_pairs={{0,1},{1,2},{2,3},{3,4},{4,5},{5,6},{6,7},{7,8},{8,9},{9,10},{10,1... | collective-permute-start | bytes 393224 | tf_op jit(solution)/shard_map/ppermute | solution.py:60
  101.6 7.1 %collective-permute-start.13 = (bf16[2,2,32,512]{3,2,1,0:T(8,128)(2,1)S(1)}, bf16[2,2,32,512]{3,2,1,0:T(8,128)(2,1)S(1)}, u32[]{:S(2)}, u32[]{:S(2)}) collective-permute-start(bf16[2,2,32,512]{3,2,1,0:T(8,128)(2,1)S(1)} %collective-permute-done.12), channel_id=1, source_target_pairs={{0,1},{1,2},{2,3},{3,4},{4,5},{5,6},{6,7},{7,8},{8,9},{9,10},{10,1... | collective-permute-start | bytes 393224 | tf_op jit(solution)/shard_map/ppermute | solution.py:60
  108.7 7.1 %collective-permute-start.14 = (bf16[2,2,32,512]{3,2,1,0:T(8,128)(2,1)S(1)}, bf16[2,2,32,512]{3,2,1,0:T(8,128)(2,1)S(1)}, u32[]{:S(2)}, u32[]{:S(2)}) collective-permute-start(bf16[2,2,32,512]{3,2,1,0:T(8,128)(2,1)S(1)} %collective-permute-done.13), channel_id=1, source_target_pairs={{0,1},{1,2},{2,3},{3,4},{4,5},{5,6},{6,7},{7,8},{8,9},{9,10},{10,1... | collective-permute-start | bytes 393224 | tf_op jit(solution)/shard_map/ppermute | solution.py:60
  116.7 10.5 %collective-permute-start.15 = (bf16[2,2,512,16]{3,2,1,0:T(8,128)(2,1)S(1)}, bf16[2,2,512,16]{3,2,1,0:T(8,128)(2,1)S(1)}, u32[]{:S(2)}, u32[]{:S(2)}) collective-permute-start(bf16[2,2,512,16]{3,2,1,0:T(8,128)(2,1)S(1)} %get-tuple-element.122), channel_id=1, source_target_pairs={{0,16},{1,17},{2,18},{3,19},{4,20},{5,21},{6,22},{7,23},{8,24},{9,... | collective-permute-start | bytes 196616 | tf_op jit(solution)/shard_map/ppermute | solution.py:14
  120.6 11.1 %collective-permute-start.16 = (bf16[2,2,512,16]{3,2,1,0:T(8,128)(2,1)S(1)}, bf16[2,2,512,16]{3,2,1,0:T(8,128)(2,1)S(1)}, u32[]{:S(2)}, u32[]{:S(2)}) collective-permute-start(bf16[2,2,512,16]{3,2,1,0:T(8,128)(2,1)S(1)} %get-tuple-element.123), channel_id=1, source_target_pairs={{16,0},{17,1},{18,2},{19,3},{20,4},{21,5},{22,6},{23,7},{24,8},{25... | collective-permute-start | bytes 196616 | tf_op jit(solution)/shard_map/ppermute | solution.py:17
Sparse Core Ops, SparseCore 0:
  425.9 89.9 all-reduce.2
